TPU v7x, 32 devices: a whole 2x2x4 slice. The times are simulated.
32 devices in a mesh: dp: 16 (over z, x, core), tp: 2 (over y).
Axes of the slice: x: 2, y: 2, z: 4, core: 2. Of those that a mesh axis runs over, the one named last changes fastest.
Arguments:
- inputs: bfloat16 [32768, 640], P('dp'), may hold values from -6 to 6
- out_grad: bfloat16 [32768, 640], P('dp'), may hold values from -6 to 6
- segment_ids: int32 [32, 1024], P('dp'), may hold values from 0 to 5, never falling along the last dimension, each value on 1 to 400 neighbouring positions
- attn_weights: float32 [4, 640, 640], P(None, 'dp', 'tp'), may hold values from -6 to 6
- ffn_weights: float32 [2, 640, 2560], P(None, 'dp', 'tp'), may hold values from -4 to 4
- head_bias: float32 [3, 640], P(None, 'tp'), may hold values from -1 to 1
- hidden_bias: float32 [2560], P('tp'), may hold values from -1 to 1
- norm_vectors: float32 [6, 640], replicated, may hold values from -1 to 2
- attn_first: float32 [4, 640, 640], P(None, 'dp', 'tp')
- ffn_first: float32 [2, 640, 2560], P(None, 'dp', 'tp')
- head_first: float32 [3, 640], P(None, 'tp')
- hidden_first: float32 [2560], P('tp')
- vector_first: float32 [6, 640], replicated
- attn_second: float32 [4, 640, 640], P(None, 'dp', 'tp')
- ffn_second: float32 [2, 640, 2560], P(None, 'dp', 'tp')
- head_second: float32 [3, 640], P(None, 'tp')
- hidden_second: float32 [2560], P('tp')
- vector_second: float32 [6, 640], replicated
Outputs:
- layer_output: bfloat16 [32768, 640], P('dp')
- input_grad: bfloat16 [32768, 640], P('dp')
- new_attn_weights: float32 [4, 640, 640], P(None, 'dp', 'tp')
- new_ffn_weights: float32 [2, 640, 2560], P(None, 'dp', 'tp')
- new_head_bias: float32 [3, 640], P(None, 'tp')
- new_hidden_bias: float32 [2560], P('tp')
- new_norm_vectors: float32 [6, 640], replicated
- attn_first_new: float32 [4, 640, 640], P(None, 'dp', 'tp')
- ffn_first_new: float32 [2, 640, 2560], P(None, 'dp', 'tp')
- head_first_new: float32 [3, 640], P(None, 'tp')
- hidden_first_new: float32 [2560], P('tp')
- vector_first_new: float32 [6, 640], replicated
- attn_second_new: float32 [3, 640, 640], P(None, 'dp', 'tp')
- out_second_new: float32 [640, 640], P('dp', 'tp')
- ffn_second_new: float32 [2, 640, 2560], P(None, 'dp', 'tp')
- head_second_new: float32 [3, 640], P(None, 'tp')
- hidden_second_new: float32 [2560], P('tp')
- vector_second_new: float32 [4, 640], replicated
- norm_second_new: float32 [2, 640], replicated
- trust_norms: float32 [2, 16], replicated
Inputs may be any that keep to these rules, and one draw needn't show every extreme that they name: `segment_ids`: within each row of 1024 slots the ids never fall; each of the 6 ids forms one run of 1 to 400 slots, and one run has exactly 400 slots.
All inputs are finite; a program needn't handle non-finite values.
Results may differ from a plain program's by a relative error of at most 0.019.
Values may be sent and summed in bfloat16 or wider, within the bound.
No kernel may reach another device: no remote copies, remote signals or barrier semaphores. Data moves between devices by JAX's collectives and lax.ppermute only.
A program may use at most 192 MiB of HBM per device.

v0:
```python
from functools import partial
import jax
import jax.numpy as jnp
from jax import lax
from jax.sharding import PartitionSpec as P

HD = 32
STEP = 10
EPS_NORM = 1e-05
EPS_ADAM = 1e-06
BETA_ONE = 0.9
BETA_TWO = 0.999
DECAY = 0.01
RATE = 0.5
MASKED = -1e30


def layer_norm(values, scale_gain, offset):
    average = jnp.mean(values, axis=-1, keepdims=True)
    centered = values - average
    variance = jnp.mean(centered * centered, axis=-1, keepdims=True)
    return centered * lax.rsqrt(variance + EPS_NORM) * scale_gain + offset


def rope_tables(segments):
    slots_index = jnp.arange(segments.shape[0], dtype=jnp.int32)
    before = jnp.sum((segments[None, :] < segments[:, None]).astype(jnp.int32), axis=1)
    position = (slots_index - before).astype(jnp.float32)
    frequency = 10000.0 ** (-jnp.arange(0, HD, 2).astype(jnp.float32) / HD)
    angles = position[:, None] * frequency[None, :]
    angles = jnp.concatenate([angles, angles], axis=-1)
    return (jnp.cos(angles), jnp.sin(angles))


def rotate(values, cosine_table, sine_table):
    middle = values.shape[-1] // 2
    turned = jnp.concatenate([-values[..., middle:], values[..., :middle]], axis=-1)
    return values * cosine_table + turned * sine_table


def block_scores(queries, keys_row, same_protein):
    scores = jnp.einsum(
        "qhd,khd->hqk", queries, keys_row, preferred_element_type=jnp.float32
    ) * HD ** (-0.5)
    return jnp.where(same_protein[None], scores, MASKED)


def attend_block(queries, keys_row, values_row, same_protein):
    scores = block_scores(queries, keys_row, same_protein)
    highest = jnp.max(scores, axis=-1, keepdims=True)
    weights_exp = jnp.exp(scores - highest)
    row_total = jnp.sum(weights_exp, axis=-1, keepdims=True)
    attention = (weights_exp / row_total).astype(jnp.bfloat16)
    heads_out = jnp.einsum(
        "hqk,khd->qhd", attention, values_row, preferred_element_type=jnp.float32
    )
    return (heads_out, (highest + jnp.log(row_total))[..., 0])


def attend_block_back(queries, keys_row, values_row, same_protein, log_total, grad_heads):
    scores = block_scores(queries, keys_row, same_protein)
    attention = jnp.exp(scores - log_total[..., None])
    grad_values = jnp.einsum(
        "hqk,qhd->khd",
        attention.astype(jnp.bfloat16),
        grad_heads,
        preferred_element_type=jnp.float32,
    )
    grad_attention = jnp.einsum(
        "qhd,khd->hqk", grad_heads, values_row, preferred_element_type=jnp.float32
    )
    center = jnp.sum(attention * grad_attention, axis=-1, keepdims=True)
    grad_scores = (attention * (grad_attention - center)).astype(jnp.bfloat16)
    grad_queries = jnp.einsum(
        "hqk,khd->qhd", grad_scores, keys_row, preferred_element_type=jnp.float32
    ) * HD ** (-0.5)
    grad_keys = jnp.einsum(
        "hqk,qhd->khd", grad_scores, queries, preferred_element_type=jnp.float32
    ) * HD ** (-0.5)
    return (grad_queries, grad_keys, grad_values)


def attend_row(queries, keys_row, values_row, segments, block_rows):
    blocks = segments.shape[0] // block_rows
    query_blocks = queries.reshape((blocks, block_rows) + queries.shape[1:])
    segment_blocks = segments.reshape(blocks, block_rows)

    def one_block(packed):
        same_protein = packed[1][:, None] == segments[None, :]
        return attend_block(packed[0], keys_row, values_row, same_protein)

    heads_out, log_total = lax.map(one_block, (query_blocks, segment_blocks))
    return (heads_out.reshape(queries.shape), log_total)


def attend_row_back(queries, keys_row, values_row, segments, log_total, grad_heads, block_rows):
    blocks = segments.shape[0] // block_rows
    query_blocks = queries.reshape((blocks, block_rows) + queries.shape[1:])
    grad_blocks = grad_heads.reshape((blocks, block_rows) + grad_heads.shape[1:])
    segment_blocks = segments.reshape(blocks, block_rows)

    def one_block(totals, packed):
        same_protein = packed[1][:, None] == segments[None, :]
        grad_queries, grad_keys, grad_values = attend_block_back(
            packed[0], keys_row, values_row, same_protein, packed[2], packed[3]
        )
        return ((totals[0] + grad_keys, totals[1] + grad_values), grad_queries)

    zeros_rows = jnp.zeros(keys_row.shape, jnp.float32)
    sums_kv, grad_queries = lax.scan(
        one_block, (zeros_rows, zeros_rows), (query_blocks, segment_blocks, log_total, grad_blocks)
    )
    return (grad_queries.reshape(queries.shape), sums_kv[0], sums_kv[1])


def lamb_moments(weight, gradient, moment_one, moment_two):
    first_new = BETA_ONE * moment_one + (1.0 - BETA_ONE) * gradient
    second_new = BETA_TWO * moment_two + (1.0 - BETA_TWO) * gradient * gradient
    corrected = first_new / (1.0 - BETA_ONE**STEP)
    variance = second_new / (1.0 - BETA_TWO**STEP)
    update = corrected / (jnp.sqrt(variance) + EPS_ADAM) + DECAY * weight
    return (first_new, second_new, update)


def sum_squares(array):
    return jnp.sum(array * array, axis=tuple(range(1, array.ndim)))


def on_device(
    inputs,
    out_grad,
    segment_ids,
    attn_weights,
    ffn_weights,
    head_bias,
    hidden_bias,
    norm_vectors,
    attn_first,
    ffn_first,
    head_first,
    hidden_first,
    vector_first,
    attn_second,
    ffn_second,
    head_second,
    hidden_second,
    vector_second,
):
    data_count = lax.axis_size("dp")
    tensor_count = lax.axis_size("tp")
    row_count, slot_count = segment_ids.shape
    token_count = row_count * slot_count
    head_width = attn_weights.shape[2]
    local_heads = head_width // HD
    block_rows = min(512, slot_count)
    shard_rows = attn_weights.shape[1]
    masters = [attn_weights, ffn_weights, head_bias, hidden_bias.reshape(1, -1), norm_vectors]
    replicas = [1.0, 1.0, 1.0 / data_count, 1.0 / data_count, 1.0 / (data_count * tensor_count)]
    weight_terms = jnp.concatenate(
        [sum_squares(masters[member]) * replicas[member] for member in range(5)]
    )
    weight_sums = lax.psum(weight_terms, ("dp", "tp"))
    gathered_attn, gathered_ffn = (
        lax.all_gather(attn_weights.astype(jnp.bfloat16), "dp", axis=1, tiled=True),
        lax.all_gather(ffn_weights.astype(jnp.bfloat16), "dp", axis=1, tiled=True),
    )
    tables = jax.vmap(rope_tables)(segment_ids)
    cosine_table = tables[0][:, :, None, :]
    sine_table = tables[1][:, :, None, :]
    features = inputs.astype(jnp.float32)
    normed, norm_back = jax.vjp(layer_norm, features, norm_vectors[0], norm_vectors[1])
    normed_low = normed.astype(jnp.bfloat16)
    projected = jnp.einsum(
        "td,cdw->ctw", normed_low, gathered_attn[:3], preferred_element_type=jnp.float32
    )
    projected = projected + head_bias[:, None, :]
    shaped = projected.reshape(3, row_count, slot_count, local_heads, HD)
    turned, rotate_back = jax.vjp(lambda pair: rotate(pair, cosine_table, sine_table), shaped[:2])
    turned_low = turned.astype(jnp.bfloat16)
    values_low = shaped[2].astype(jnp.bfloat16)
    heads_out, log_total = lax.map(
        lambda packed: attend_row(packed[0], packed[1], packed[2], packed[3], block_rows),
        (turned_low[0], turned_low[1], values_low, segment_ids),
    )
    heads_low = heads_out.reshape(token_count, head_width).astype(jnp.bfloat16)
    out_projection = gathered_attn[3]
    attended = lax.psum(
        jnp.einsum(
            "tw,dw->td", heads_low, out_projection, preferred_element_type=jnp.float32
        ).astype(jnp.bfloat16),
        "tp",
    ).astype(jnp.float32)
    residual = features + attended + norm_vectors[2]
    normed_two, norm_two_back = jax.vjp(layer_norm, residual, norm_vectors[3], norm_vectors[4])
    normed_two_low = normed_two.astype(jnp.bfloat16)
    preact = (
        jnp.dot(normed_two_low, gathered_ffn[0], preferred_element_type=jnp.float32) + hidden_bias
    )
    activated, gelu_back = jax.vjp(partial(jax.nn.gelu, approximate=False), preact)
    activated_low = activated.astype(jnp.bfloat16)
    mixed_sum = lax.psum(
        jnp.einsum(
            "tf,df->td", activated_low, gathered_ffn[1], preferred_element_type=jnp.float32
        ).astype(jnp.bfloat16),
        "tp",
    ).astype(jnp.float32)
    layer_output = (residual + mixed_sum + norm_vectors[5]).astype(jnp.bfloat16)
    grad_output = out_grad.astype(jnp.float32)
    grad_down = jnp.einsum("td,tf->df", out_grad, activated_low, preferred_element_type=jnp.float32)
    grad_act = jnp.einsum(
        "td,df->tf", out_grad, gathered_ffn[1], preferred_element_type=jnp.float32
    )
    grad_pre = gelu_back(grad_act)[0].astype(jnp.bfloat16)
    grad_up = jnp.einsum("td,tf->df", normed_two_low, grad_pre, preferred_element_type=jnp.float32)
    grad_hidden_bias = jnp.sum(grad_pre.astype(jnp.float32), axis=0)
    grad_normed_two = lax.psum(
        jnp.einsum(
            "tf,df->td", grad_pre, gathered_ffn[0], preferred_element_type=jnp.float32
        ).astype(jnp.bfloat16),
        "tp",
    ).astype(jnp.float32)
    grad_residual_ln, grad_gain_two, grad_shift_two = norm_two_back(grad_normed_two)
    grad_residual = grad_output + grad_residual_ln
    grad_residual_low = grad_residual.astype(jnp.bfloat16)
    grad_out_projection = jnp.einsum(
        "td,tw->dw", grad_residual_low, heads_low, preferred_element_type=jnp.float32
    )
    grad_heads = jnp.einsum(
        "td,dw->tw", grad_residual_low, out_projection, preferred_element_type=jnp.float32
    )
    grad_heads = grad_heads.astype(jnp.bfloat16).reshape(row_count, slot_count, local_heads, HD)
    grad_turned_q, grad_turned_k, grad_values = lax.map(
        lambda packed: attend_row_back(
            packed[0], packed[1], packed[2], packed[3], packed[4], packed[5], block_rows
        ),
        (turned_low[0], turned_low[1], values_low, segment_ids, log_total, grad_heads),
    )
    grad_shaped_qk = rotate_back(jnp.stack([grad_turned_q, grad_turned_k]))[0]
    grad_projected = jnp.concatenate([grad_shaped_qk, grad_values[None]], axis=0)
    grad_projected = grad_projected.reshape(3, token_count, head_width).astype(jnp.bfloat16)
    grad_head_bias = jnp.sum(grad_projected.astype(jnp.float32), axis=1)
    grad_qkv = jnp.einsum(
        "td,ctw->cdw", normed_low, grad_projected, preferred_element_type=jnp.float32
    )
    grad_normed = lax.psum(
        jnp.einsum(
            "ctw,cdw->td", grad_projected, gathered_attn[:3], preferred_element_type=jnp.float32
        ).astype(jnp.bfloat16),
        "tp",
    ).astype(jnp.float32)
    grad_features_ln, grad_gain, grad_shift = norm_back(grad_normed)
    input_grad = (grad_residual + grad_features_ln).astype(jnp.bfloat16)
    grad_vectors = jnp.stack(
        [
            grad_gain,
            grad_shift,
            jnp.sum(grad_residual, axis=0),
            grad_gain_two,
            grad_shift_two,
            jnp.sum(grad_output, axis=0),
        ]
    )
    grad_attn = jnp.concatenate([grad_qkv, grad_out_projection[None]], axis=0)
    grad_ffn = jnp.stack([grad_up, grad_down])
    full_attn, full_ffn, sum_head, sum_hidden, sum_vectors = lax.psum(
        (grad_attn, grad_ffn, grad_head_bias, grad_hidden_bias, grad_vectors), "dp"
    )
    offset_rows = lax.axis_index("dp") * shard_rows
    own_attn = lax.dynamic_slice_in_dim(full_attn, offset_rows, shard_rows, 1)
    own_ffn = lax.dynamic_slice_in_dim(full_ffn, offset_rows, shard_rows, 1)
    grads_list = [own_attn, own_ffn, sum_head, sum_hidden.reshape(1, -1), sum_vectors]
    firsts = [attn_first, ffn_first, head_first, hidden_first.reshape(1, -1), vector_first]
    seconds = [attn_second, ffn_second, head_second, hidden_second.reshape(1, -1), vector_second]
    results = [
        lamb_moments(masters[member], grads_list[member], firsts[member], seconds[member])
        for member in range(5)
    ]
    update_terms = jnp.concatenate(
        [sum_squares(results[member][2]) * replicas[member] for member in range(5)]
    )
    update_sums = lax.psum(update_terms, ("dp", "tp"))
    weight_norms = jnp.sqrt(weight_sums)
    update_norms = jnp.sqrt(update_sums)
    trust_ratio = weight_norms / update_norms
    counts = [4, 2, 3, 1, 6]
    new_weights = []
    begin_at = 0
    for member in range(5):
        piece_ratio = trust_ratio[begin_at : begin_at + counts[member]]
        shaped_ratio = piece_ratio.reshape((-1,) + (1,) * (masters[member].ndim - 1))
        new_weights.append(masters[member] - RATE * shaped_ratio * results[member][2])
        begin_at += counts[member]
    return (
        layer_output,
        input_grad,
        new_weights[0],
        new_weights[1],
        new_weights[2],
        new_weights[3].reshape(-1),
        new_weights[4],
        results[0][0],
        results[1][0],
        results[2][0],
        results[3][0].reshape(-1),
        results[4][0],
        results[0][1][:3],
        results[0][1][3],
        results[1][1],
        results[2][1],
        results[3][1].reshape(-1),
        results[4][1][2:],
        results[4][1][:2],
        jnp.stack([weight_norms, update_norms]),
    )


def solution(mesh):
    in_specs = (
        P("dp", None),
        P("dp", None),
        P("dp", None),
        P(None, "dp", "tp"),
        P(None, "dp", "tp"),
        P(None, "tp"),
        P("tp"),
        P(),
        P(None, "dp", "tp"),
        P(None, "dp", "tp"),
        P(None, "tp"),
        P("tp"),
        P(),
        P(None, "dp", "tp"),
        P(None, "dp", "tp"),
        P(None, "tp"),
        P("tp"),
        P(),
    )
    out_specs = (
        P("dp", None),
        P("dp", None),
        P(None, "dp", "tp"),
        P(None, "dp", "tp"),
        P(None, "tp"),
        P("tp"),
        P(),
        P(None, "dp", "tp"),
        P(None, "dp", "tp"),
        P(None, "tp"),
        P("tp"),
        P(),
        P(None, "dp", "tp"),
        P("dp", "tp"),
        P(None, "dp", "tp"),
        P(None, "tp"),
        P("tp"),
        P(),
        P(),
        P(),
    )
    return jax.shard_map(
        on_device, mesh=mesh, in_specs=in_specs, out_specs=out_specs, check_vma=False
    )
```

profile of v0, /device:TPU:12, one launch (start us, length us, event | category | flops | bytes accessed | tf_op | source)
XLA Modules:
  0.0 1304.4 jit_solution(11081138493760027001)
XLA Ops:
  17.8 34.1 %all-gather.3.cloned.1.call-done = bf16[4,640,320]{2,0,1:T(4,128)(2,1)} async-done(((bf16[4,40,320]{2,0,1:T(4,128)(2,1)}), bf16[4,640,320]{2,0,1:T(4,128)(2,1)}) %all-gather.3.cloned.1.call-update) | async-done | bytes 1638416 | tf_op jit(solution)/shard_map/all_gather | solution.py:164
  88.0 138.8 %while.54 = (s32[]{:T(128)}, bf16[2,1024,10,32]{3,2,1,0:T(8,128)(2,1)}, f32[2,2,10,512]{3,2,1,0:T(8,128)}, bf16[2,1024,10,32]{1,3,2,0:T(8,128)(2,1)S(1)}, s32[2,...) while((s32[]{:T(128)}, ...), condition=%wide.region_8.0_spmd, body=%wide.region_3.8_spmd.sunk | while | flops 734522368 | bytes 181594624 | solution.py:181
  92.8 54.8 %while.57 = (s32[]{:T(128)}, bf16[2,512,10,32]{1,3,2,0:T(8,128)(2,1)S(1)}, f32[2,10,512]{2,1,0:T(8,128)S(1)}, s32[2,512]{1,0:T(2,128)S(1)}, s32[1024]{0:T(1024)S...) while((s32[]{:T(128)}, ...), condition=%wide.region_7.7_spmd, body=%wide.region_4.6_spmd.sunk | while | flops 734522368 | bytes 154048688 | solution.py:92
  162.2 54.8 %while.57 = (s32[]{:T(128)}, bf16[2,512,10,32]{1,3,2,0:T(8,128)(2,1)S(1)}, f32[2,10,512]{2,1,0:T(8,128)S(1)}, s32[2,512]{1,0:T(2,128)S(1)}, s32[1024]{0:T(1024)S...) while((s32[]{:T(128)}, ...), condition=%wide.region_7.7_spmd, body=%wide.region_4.6_spmd.sunk | while | flops 734522368 | bytes 154048688 | solution.py:92
  243.5 72.7 %all-reduce.11.cloned.1.call-done = bf16[2048,640]{1,0:T(8,128)(2,1)} async-done(((bf16[2048,640]{1,0:T(8,128)(2,1)}), bf16[2048,640]{1,0:T(8,128)(2,1)}) %all-reduce.11.cloned.1.call-update) | async-done | bytes 2621456 | tf_op jit(solution)/shard_map/psum | solution.py:187
  320.5 46.1 %all-gather.5.cloned.1.call-done = bf16[2,640,1280]{2,1,0:T(8,128)(2,1)} async-done(((bf16[2,40,1280]{2,1,0:T(8,128)(2,1)}), bf16[2,640,1280]{2,1,0:T(8,128)(2,1)}) %all-gather.5.cloned.1.call-update) | async-done | bytes 3276816 | tf_op jit(solution)/shard_map/all_gather | solution.py:165
  366.6 31.1 %multiply_convert_fusion.1 = (bf16[2048,1280]{1,0:T(8,128)(2,1)}, f32[2048,1280]{1,0:T(8,128)}, f32[2048,1280]{1,0:T(8,128)}) fusion(f32[1280]{0:T(1024)S(1)} %copy-done.50, bf16[2,640,1280]{2,1,0:T(8,128)(2,1)} %all-gather.5.cloned.1.call-done, f32[640]{0:T(1024)S(1)} %copy-done.58, f32[640]{0:T(1024)S(1)} %copy-done.47, f32[2048]{0:T(1024)S(1)} %fusion.84, ...), kind=kOutput, calls=%fused_computation.69 | convolution fusion | flops 3540254720 | bytes 33124864 | tf_op jit(solution)/shard_map/dot_general | solution.py:197
  397.8 12.4 convert_reduce_fusion
  433.5 56.9 %all-reduce.13.cloned.1.call-done = bf16[2048,640]{1,0:T(8,128)(2,1)} async-done(((bf16[2048,640]{1,0:T(8,128)(2,1)}), bf16[2048,640]{1,0:T(8,128)(2,1)}) %all-reduce.13.cloned.1.call-update) | async-done | bytes 2621456 | tf_op jit(solution)/shard_map/psum | solution.py:216
  510.4 277.2 %while.56 = (s32[]{:T(128)}, f32[2,1024,10,32]{1,3,2,0:T(8,128)}, f32[2,1024,10,32]{1,3,2,0:T(8,128)}, bf16[2,1024,10,32]{1,3,2,0:T(8,128)(2,1)}, bf16[2,1024,10...) while((s32[]{:T(128)}, f32[2,1024,10,32]{1,3,2,0:T(8,128)}, ...), condition=%wide.region_20.21_spmd, body=%wide.region_16.20_spmd.sunk | while | flops 1758686208 | bytes 284158464 | solution.py:232
  522.2 111.2 %while.58 = (s32[]{:T(128)}, f32[1024,10,32]{0,2,1:T(8,128)S(1)}, f32[1024,10,32]{0,2,1:T(8,128)}, f32[2,512,10,32]{1,3,2,0:T(8,128)}, bf16[2,512,10,32]{1,3,2,0...) while((s32[]{:T(128)}, f32[1024,10,32]{0,2,1:T(8,128)S(1)}, ...), condition=%wide.region_19.19_spmd.clone, body=%wide.region_17.18_spmd.clone.sunk | while | flops 1758686208 | bytes 255219920 | solution.py:110
  541.9 15.2 %multiply_reduce_fusion.13 = (f32[10,512]{1,0:T(8,128)S(1)}, f32[10,512,1024]{2,1,0:T(8,128)}) fusion(f32[10,512,1024]{2,1,0:T(8,128)} %copy-done, f32[10,512]{1,0:T(8,128)S(1)} %dynamic-slice_bitcast_fusion.15, pred[512,1024]{1,0:T(8,128)(4,1)S(1)} %broadcast_compare_fusion.4, bf16[1024,10,32]{0,2,1:T(8,128)(2,1)} %get-tuple-element.1035, ...), kind=kOutput, calls=%fused_computation.18.clone.1 | convolution fusion | flops 361753600 | bytes 43491332 | tf_op jit(solution)/shard_map/while/body/eval_jaxpr/while/body/eval_jaxpr/qhd,khd->hqk/dot_general | solution.py:69
  557.0 14.6 %multiply_convert_fusion.3 = bf16[10,512,1024]{2,1,0:T(8,128)(2,1)S(1)} fusion(f32[10,512,1024]{2,1,0:T(8,128)} %get-tuple-element.987, f32[10,512,1024]{2,1,0:T(8,128)} %copy-done, f32[10,512]{1,0:T(8,128)S(1)} %get-tuple-element.988, f32[10,512]{1,0:T(8,128)S(1)} %dynamic-slice_bitcast_fusion.15, pred[512,1024]{1,0:T(8,128)(4,1)S(1)} %broadcast_compare_fusion.4), kind=kLoop, calls=%fused_computation.17.clone.1 | loop fusion | flops 31457280 | bytes 52994048 | tf_op jit(solution)/shard_map/while/body/eval_jaxpr/while/body/eval_jaxpr/convert_element_type | solution.py:73
  597.6 15.2 %multiply_reduce_fusion.13 = (f32[10,512]{1,0:T(8,128)S(1)}, f32[10,512,1024]{2,1,0:T(8,128)}) fusion(f32[10,512,1024]{2,1,0:T(8,128)} %copy-done, f32[10,512]{1,0:T(8,128)S(1)} %dynamic-slice_bitcast_fusion.15, pred[512,1024]{1,0:T(8,128)(4,1)S(1)} %broadcast_compare_fusion.4, bf16[1024,10,32]{0,2,1:T(8,128)(2,1)} %get-tuple-element.1035, ...), kind=kOutput, calls=%fused_computation.18.clone.1 | convolution fusion | flops 361753600 | bytes 43491332 | tf_op jit(solution)/shard_map/while/body/eval_jaxpr/while/body/eval_jaxpr/qhd,khd->hqk/dot_general | solution.py:69
  612.8 14.6 %multiply_convert_fusion.3 = bf16[10,512,1024]{2,1,0:T(8,128)(2,1)S(1)} fusion(f32[10,512,1024]{2,1,0:T(8,128)} %get-tuple-element.987, f32[10,512,1024]{2,1,0:T(8,128)} %copy-done, f32[10,512]{1,0:T(8,128)S(1)} %get-tuple-element.988, f32[10,512]{1,0:T(8,128)S(1)} %dynamic-slice_bitcast_fusion.15, pred[512,1024]{1,0:T(8,128)(4,1)S(1)} %broadcast_compare_fusion.4), kind=kLoop, calls=%fused_computation.17.clone.1 | loop fusion | flops 31457280 | bytes 52994048 | tf_op jit(solution)/shard_map/while/body/eval_jaxpr/while/body/eval_jaxpr/convert_element_type | solution.py:73
  660.5 111.2 %while.58 = (s32[]{:T(128)}, f32[1024,10,32]{0,2,1:T(8,128)S(1)}, f32[1024,10,32]{0,2,1:T(8,128)}, f32[2,512,10,32]{1,3,2,0:T(8,128)}, bf16[2,512,10,32]{1,3,2,0...) while((s32[]{:T(128)}, f32[1024,10,32]{0,2,1:T(8,128)S(1)}, ...), condition=%wide.region_19.19_spmd.clone, body=%wide.region_17.18_spmd.clone.sunk | while | flops 1758686208 | bytes 255219920 | solution.py:110
  680.2 15.2 %multiply_reduce_fusion.13 = (f32[10,512]{1,0:T(8,128)S(1)}, f32[10,512,1024]{2,1,0:T(8,128)}) fusion(f32[10,512,1024]{2,1,0:T(8,128)} %copy-done, f32[10,512]{1,0:T(8,128)S(1)} %dynamic-slice_bitcast_fusion.15, pred[512,1024]{1,0:T(8,128)(4,1)S(1)} %broadcast_compare_fusion.4, bf16[1024,10,32]{0,2,1:T(8,128)(2,1)} %get-tuple-element.1035, ...), kind=kOutput, calls=%fused_computation.18.clone.1 | convolution fusion | flops 361753600 | bytes 43491332 | tf_op jit(solution)/shard_map/while/body/eval_jaxpr/while/body/eval_jaxpr/qhd,khd->hqk/dot_general | solution.py:69
  695.3 14.6 %multiply_convert_fusion.3 = bf16[10,512,1024]{2,1,0:T(8,128)(2,1)S(1)} fusion(f32[10,512,1024]{2,1,0:T(8,128)} %get-tuple-element.987, f32[10,512,1024]{2,1,0:T(8,128)} %copy-done, f32[10,512]{1,0:T(8,128)S(1)} %get-tuple-element.988, f32[10,512]{1,0:T(8,128)S(1)} %dynamic-slice_bitcast_fusion.15, pred[512,1024]{1,0:T(8,128)(4,1)S(1)} %broadcast_compare_fusion.4), kind=kLoop, calls=%fused_computation.17.clone.1 | loop fusion | flops 31457280 | bytes 52994048 | tf_op jit(solution)/shard_map/while/body/eval_jaxpr/while/body/eval_jaxpr/convert_element_type | solution.py:73
  735.9 15.2 %multiply_reduce_fusion.13 = (f32[10,512]{1,0:T(8,128)S(1)}, f32[10,512,1024]{2,1,0:T(8,128)}) fusion(f32[10,512,1024]{2,1,0:T(8,128)} %copy-done, f32[10,512]{1,0:T(8,128)S(1)} %dynamic-slice_bitcast_fusion.15, pred[512,1024]{1,0:T(8,128)(4,1)S(1)} %broadcast_compare_fusion.4, bf16[1024,10,32]{0,2,1:T(8,128)(2,1)} %get-tuple-element.1035, ...), kind=kOutput, calls=%fused_computation.18.clone.1 | convolution fusion | flops 361753600 | bytes 43491332 | tf_op jit(solution)/shard_map/while/body/eval_jaxpr/while/body/eval_jaxpr/qhd,khd->hqk/dot_general | solution.py:69
  751.1 14.6 %multiply_convert_fusion.3 = bf16[10,512,1024]{2,1,0:T(8,128)(2,1)S(1)} fusion(f32[10,512,1024]{2,1,0:T(8,128)} %get-tuple-element.987, f32[10,512,1024]{2,1,0:T(8,128)} %copy-done, f32[10,512]{1,0:T(8,128)S(1)} %get-tuple-element.988, f32[10,512]{1,0:T(8,128)S(1)} %dynamic-slice_bitcast_fusion.15, pred[512,1024]{1,0:T(8,128)(4,1)S(1)} %broadcast_compare_fusion.4), kind=kLoop, calls=%fused_computation.17.clone.1 | loop fusion | flops 31457280 | bytes 52994048 | tf_op jit(solution)/shard_map/while/body/eval_jaxpr/while/body/eval_jaxpr/convert_element_type | solution.py:73
  837.5 182.1 %all-reduce.15.cloned.1.call-done = (f32[4,640,320]{2,1,0:T(8,128)}, f32[2,640,1280]{2,1,0:T(8,128)}) async-done(((f32[4,640,320]{2,1,0:T(8,128)}, f32[2,640,1280]{2,1,0:T(8,128)}), (f32[4,640,320]{2,1,0:T(8,128)}, f32[2,640,1280]{2,1,0:T(8,128)})) %all-reduce.15.cloned.1.call-update) | async-done | bytes 9830416 | tf_op jit(solution)/shard_map/psum | solution.py:265
  1025.9 126.9 %all-reduce.17.cloned.1.call-done = (bf16[2048,640]{1,0:T(8,128)(2,1)}, bf16[2048,640]{1,0:T(8,128)(2,1)}) async-done(((bf16[2048,640]{1,0:T(8,128)(2,1)}, bf16[2048,640]{1,0:T(8,128)(2,1)}), (bf16[2048,640]{1,0:T(8,128)(2,1)}, bf16[2048,640]{1,0:T(8,128)(2,1)})) %all-reduce.17.cloned.1.call-update) | async-done | bytes 5242896 | tf_op jit(solution)/shard_map/psum | solution.py:201
  1161.9 54.0 %all-reduce.3 = (f32[3,320]{1,0:T(4,128)}, f32[1280]{0:T(1024)}, f32[6,640]{1,0:T(8,128)}) all-reduce(f32[3,320]{1,0:T(4,128)} %convert_reduce_fusion.2, f32[1280]{0:T(1024)} %get-tuple-element.699, f32[6,640]{1,0:T(8,128)S(1)} %stack.48), channel_id=1, replica_groups=mesh['dp'=16,'tp'=2] {'dp'}, use_global_device_ids=true, to_apply=%region_35.36 | all-reduce | flops 6080 | bytes 48640 | tf_op jit(solution)/shard_map/psum | solution.py:265
  1226.4 48.9 %all-reduce.2 = (f32[16]{0:T(128)}, f32[16]{0:T(128)}) all-reduce(f32[16]{0:T(128)} %concatenate.39, f32[16]{0:T(128)} %concatenate.37), channel_id=1, replica_groups=mesh['dp'=16,'tp'=2] {'dp','tp'}, use_global_device_ids=true, to_apply=%region_48.49 | all-reduce | flops 32 | bytes 256 | tf_op jit(solution)/shard_map/psum | solution.py:281
  (389 shorter events, 501.9 us)
Async XLA Ops:
  7.2 49.2 %copy-start.51 = (f32[3,320]{1,0:T(4,128)S(1)}, f32[3,320]{1,0:T(4,128)}, u32[]{:S(2)}) copy-start(f32[3,320]{1,0:T(4,128)} %param.31) | copy-start | bytes 11524
  7.2 44.7 %all-gather.3.cloned.1.call-start = ((), (), s32[]{:S(2)}) async-start(), calls=%async_computation | async-start | bytes 2088960 | tf_op jit(solution)/shard_map/all_gather | solution.py:164
  9.1 307.1 %all-reduce.11.cloned.1.call-start = ((), (), s32[]{:S(2)}) async-start(), calls=%async_computation.1 | async-start | bytes 5242880 | tf_op jit(solution)/shard_map/psum | solution.py:187
  10.8 50.4 %copy-start.48 = (f32[640]{0:T(1024)}, f32[640]{0:T(1024)S(1)}, u32[]{:S(2)}) copy-start(f32[640]{0:T(1024)S(1)} %get-tuple-element.571) | copy-start | bytes 7684
  10.8 50.4 %copy-start.56 = (f32[640]{0:T(1024)}, f32[640]{0:T(1024)S(1)}, u32[]{:S(2)}) copy-start(f32[640]{0:T(1024)S(1)} %get-tuple-element.570) | copy-start | bytes 7684
  13.8 69.5 %copy-start.29 = (f32[2,1024,32]{1,2,0:T(8,128)}, f32[2,1024,32]{1,2,0:T(8,128)S(1)}, u32[]{:S(2)}) copy-start(f32[2,1024,32]{1,2,0:T(8,128)S(1)} %get-tuple-element.692) | copy-start | bytes 786436
  13.8 69.5 %copy-start.31 = (f32[2,1024,32]{1,2,0:T(8,128)}, f32[2,1024,32]{1,2,0:T(8,128)S(1)}, u32[]{:S(2)}) copy-start(f32[2,1024,32]{1,2,0:T(8,128)S(1)} %get-tuple-element.693) | copy-start | bytes 786436
  16.2 45.1 %copy-start.38 = (f32[2048]{0:T(1024)}, f32[2048]{0:T(1024)S(1)}, u32[]{:S(2)}) copy-start(f32[2048]{0:T(1024)S(1)} %broadcast_multiply_fusion.2) | copy-start | bytes 24580
  17.8 43.4 %copy-start.43 = (f32[2048]{0:T(1024)}, f32[2048]{0:T(1024)S(1)}, u32[]{:S(2)}) copy-start(f32[2048]{0:T(1024)S(1)} %fusion.83) | copy-start | bytes 24580
  92.8 54.8 %copy-start.36 = (f32[2,2,10,512]{3,2,1,0:T(8,128)S(1)}, f32[2,2,10,512]{3,2,1,0:T(8,128)}, u32[]{:S(2)}) copy-start(f32[2,2,10,512]{3,2,1,0:T(8,128)} %get-tuple-element.1077) | copy-start | bytes 245764 | tf_op jit(solution)/shard_map/while
  162.2 54.8 %copy-start.36 = (f32[2,2,10,512]{3,2,1,0:T(8,128)S(1)}, f32[2,2,10,512]{3,2,1,0:T(8,128)}, u32[]{:S(2)}) copy-start(f32[2,2,10,512]{3,2,1,0:T(8,128)} %get-tuple-element.1077) | copy-start | bytes 245764 | tf_op jit(solution)/shard_map/while
  237.9 78.3 %copy-start.4 = (bf16[2048,640]{1,0:T(8,128)(2,1)S(1)}, bf16[2048,640]{1,0:T(8,128)(2,1)}, u32[]{:S(2)}) copy-start(bf16[2048,640]{1,0:T(8,128)(2,1)} %param.26) | copy-start | bytes 7864324
  237.9 78.3 %copy-start.40 = (f32[640]{0:T(1024)S(1)}, f32[640]{0:T(1024)}, u32[]{:S(2)}) copy-start(f32[640]{0:T(1024)} %get-tuple-element.569) | copy-start | bytes 7684
  242.7 123.9 %all-gather.5.cloned.1.call-start = ((), (), s32[]{:S(2)}) async-start(), calls=%async_computation.2 | async-start | bytes 3481600 | tf_op jit(solution)/shard_map/all_gather | solution.py:165
  243.4 247.0 %all-reduce.13.cloned.1.call-start = ((), (), s32[]{:S(2)}) async-start(), calls=%async_computation.3 | async-start | bytes 5242880 | tf_op jit(solution)/shard_map/psum | solution.py:216
  316.2 50.4 %copy-start.47 = (f32[640]{0:T(1024)S(1)}, f32[640]{0:T(1024)}, u32[]{:S(2)}) copy-start(f32[640]{0:T(1024)} %get-tuple-element.568) | copy-start | bytes 7684
  316.2 50.4 %copy-start.50 = (f32[1280]{0:T(1024)S(1)}, f32[1280]{0:T(1024)}, u32[]{:S(2)}) copy-start(f32[1280]{0:T(1024)} %param.32) | copy-start | bytes 15364
  316.2 50.4 %copy-start.58 = (f32[640]{0:T(1024)S(1)}, f32[640]{0:T(1024)}, u32[]{:S(2)}) copy-start(f32[640]{0:T(1024)} %get-tuple-element.567) | copy-start | bytes 7684
  418.5 601.2 %all-reduce.15.cloned.1.call-start = ((), (), s32[]{:S(2)}) async-start(), calls=%async_computation.4 | async-start | bytes 20971520 | tf_op jit(solution)/shard_map/psum | solution.py:265
  817.1 335.7 %all-reduce.17.cloned.1.call-start = ((), (), s32[]{:S(2)}) async-start(), calls=%async_computation.5 | async-start | bytes 10485760 | tf_op jit(solution)/shard_map/psum | solution.py:201
  831.1 188.6 %copy-start.33 = (f32[4,40,320]{2,1,0:T(8,128)S(1)}, f32[4,40,320]{2,1,0:T(8,128)}, u32[]{:S(2)}) copy-start(f32[4,40,320]{2,1,0:T(8,128)} %param.29) | copy-start | bytes 614404
  831.1 191.8 %copy-start.26 = (f32[2,40,1280]{2,1,0:T(8,128)S(1)}, f32[2,40,1280]{2,1,0:T(8,128)}, u32[]{:S(2)}) copy-start(f32[2,40,1280]{2,1,0:T(8,128)} %param.30) | copy-start | bytes 1228804
  837.5 319.3 %copy-start.46 = (f32[2048]{0:T(1024)S(1)}, f32[2048]{0:T(1024)}, u32[]{:S(2)}) copy-start(f32[2048]{0:T(1024)} %copy-done.45) | copy-start | bytes 24580
  1156.2 131.7 %copy-start.41 = (f32[640]{0:T(1024)S(1)}, f32[640]{0:T(1024)}, u32[]{:S(2)}) copy-start(f32[640]{0:T(1024)} %get-tuple-element.569) | copy-start | bytes 7684
  (63 other events, 400.9 us)
Sparse Core Ops, SparseCore 0:
  10.9 40.9 all-gather.2
  242.8 73.3 all-reduce.10
  319.2 47.3 all-gather.4
  418.6 71.8 all-reduce.12
  817.2 202.3 all-reduce.14
  1022.7 130.0 all-reduce.16
where the time goes:
time: 1320 us; the launch traced here: 1300 us
  waiting for transfers between devices  519 us (39%)
  matrix products  279 us (21%)
  local copies, waits for them, and re-layouts  218 us (17%)
  other arithmetic  167 us (13%)
  blocking collectives  103 us (8%)
  between operations  17 us (1%)
    psum x1, waiting for transfers between devices, on_device(): lax.psum((grad_attn, grad_ffn, grad_head_bias, grad_hidden_bias, grad_vec...  182 us
    psum x1, waiting for transfers between devices, on_device(): lax.psum(jnp.einsum('tf,df->td', activated_low, gathered_ffn[1], preferre...  127 us
    psum x1, waiting for transfers between devices, on_device(): lax.psum(jnp.einsum('tw,dw->td', heads_low, out_projection, preferred_ele...  72.7 us
    dot_general x4, matrix products, attend_block_back(): jnp.einsum('qhd,khd->hqk', grad_heads, values_row, preferred_element_type...  60.6 us
    while x56, local copies, waits for them, and re-layouts  59.7 us
    convert_element_type x4, other arithmetic, attend_block_back(): grad_scores = (attention * (grad_attention - center)).astype(jnp.bfloat16)  58.3 us
    psum x1, waiting for transfers between devices, on_device(): lax.psum(jnp.einsum('tf,df->td', grad_pre, gathered_ffn[0], preferred_ele...  56.9 us
    psum x1, blocking collectives, on_device(): lax.psum((grad_attn, grad_ffn, grad_head_bias, grad_hidden_bias, grad_vec...  54 us
  transfers between devices with their start and end apart: 6, of which 6 were waited for; matrix products, arithmetic and copies ran while one was open for 4% of the time, Pallas kernels for 0%

commit v1 on v0

--- a/solution.py
+++ b/solution.py
@@ -198,11 +198,14 @@
     )
     activated, gelu_back = jax.vjp(partial(jax.nn.gelu, approximate=False), preact)
     activated_low = activated.astype(jnp.bfloat16)
-    mixed_sum = lax.psum(
-        jnp.einsum(
-            "tf,df->td", activated_low, gathered_ffn[1], preferred_element_type=jnp.float32
-        ).astype(jnp.bfloat16),
-        "tp",
+    mixed_sum = jnp.sum(
+        lax.all_gather(
+            jnp.einsum(
+                "tf,df->td", activated_low, gathered_ffn[1], preferred_element_type=jnp.float32
+            ).astype(jnp.bfloat16),
+            "tp",
+        ),
+        axis=0,
     ).astype(jnp.float32)
     layer_output = (residual + mixed_sum + norm_vectors[5]).astype(jnp.bfloat16)
     grad_output = out_grad.astype(jnp.float32)

time: 1320 us -> 1240 us (0.939)
  waiting for transfers between devices: 519 us -> 449 us
    psum x1, waiting for transfers between devices: 127 us -> 48.7 us  [on_device(): lax.psum(jnp.einsum('ctw,cdw->td', grad_projected, gathered_attn[:3], pre...]
    all_gather x0 -> x1, waiting for transfers between devices: none -> 60.7 us  [on_device(): lax.all_gather(jnp.einsum('tf,df->td', activated_low, gathered_ffn[1], pr...]
    psum x1, waiting for transfers between devices: 182 us -> 133 us  [on_device(): lax.psum((grad_attn, grad_ffn, grad_head_bias, grad_hidden_bias, grad_vec...]
  transfers between devices with their start and end apart: 6 -> 7, of which waited for: 6 -> 7; matrix products, arithmetic and copies ran while one was open for 4% -> 7% of each run, Pallas kernels for 0% -> 0%
where the time goes in v1:
time: 1240 us; the launch traced here: 1230 us
  waiting for transfers between devices  449 us (36%)
  matrix products  286 us (23%)
  local copies, waits for them, and re-layouts  217 us (18%)
  other arithmetic  163 us (13%)
  blocking collectives  96.2 us (8%)
  between operations  17.4 us (1%)
    psum x1, waiting for transfers between devices, on_device(): lax.psum((grad_attn, grad_ffn, grad_head_bias, grad_hidden_bias, grad_vec...  133 us
    psum x1, waiting for transfers between devices, on_device(): lax.psum(jnp.einsum('tw,dw->td', heads_low, out_projection, preferred_ele...  72.7 us
    all_gather x1, waiting for transfers between devices, on_device(): lax.all_gather(jnp.einsum('tf,df->td', activated_low, gathered_ffn[1], pr...  60.7 us
    dot_general x4, matrix products, attend_block_back(): jnp.einsum('qhd,khd->hqk', grad_heads, values_row, preferred_element_type...  60.7 us
    while x56, local copies, waits for them, and re-layouts  59.6 us
    convert_element_type x4, other arithmetic, attend_block_back(): grad_scores = (attention * (grad_attention - center)).astype(jnp.bfloat16)  58.3 us
    psum x1, blocking collectives, on_device(): lax.psum((grad_attn, grad_ffn, grad_head_bias, grad_hidden_bias, grad_vec...  56.1 us
    psum x1, waiting for transfers between devices, on_device(): lax.psum(jnp.einsum('tf,df->td', grad_pre, gathered_ffn[0], preferred_ele...  54 us
  transfers between devices with their start and end apart: 7, of which 7 were waited for; matrix products, arithmetic and copies ran while one was open for 7% of the time, Pallas kernels for 0%

profile of v1, /device:TPU:12, one launch (start us, length us, event | category | flops | bytes accessed | tf_op | source)
XLA Modules:
  0.0 1230.3 jit_solution(10765206592842855156)
XLA Ops:
  17.8 34.1 %all-gather.5.cloned.1.call-done = bf16[4,640,320]{2,0,1:T(4,128)(2,1)} async-done(((bf16[4,40,320]{2,0,1:T(4,128)(2,1)}), bf16[4,640,320]{2,0,1:T(4,128)(2,1)}) %all-gather.5.cloned.1.call-update) | async-done | bytes 1638416 | tf_op jit(solution)/shard_map/all_gather | solution.py:164
  87.7 138.7 %while.54 = (s32[]{:T(128)}, bf16[2,1024,10,32]{3,2,1,0:T(8,128)(2,1)}, f32[2,2,10,512]{3,2,1,0:T(8,128)}, bf16[2,1024,10,32]{1,3,2,0:T(8,128)(2,1)S(1)}, s32[2,...) while((s32[]{:T(128)}, ...), condition=%wide.region_8.0_spmd, body=%wide.region_3.8_spmd.sunk | while | flops 734522368 | bytes 181594624 | solution.py:181
  92.6 54.8 %while.57 = (s32[]{:T(128)}, bf16[2,512,10,32]{1,3,2,0:T(8,128)(2,1)S(1)}, f32[2,10,512]{2,1,0:T(8,128)S(1)}, s32[2,512]{1,0:T(2,128)S(1)}, s32[1024]{0:T(1024)S...) while((s32[]{:T(128)}, ...), condition=%wide.region_7.7_spmd, body=%wide.region_4.6_spmd.sunk | while | flops 734522368 | bytes 154048688 | solution.py:92
  161.9 54.8 %while.57 = (s32[]{:T(128)}, bf16[2,512,10,32]{1,3,2,0:T(8,128)(2,1)S(1)}, f32[2,10,512]{2,1,0:T(8,128)S(1)}, s32[2,512]{1,0:T(2,128)S(1)}, s32[1024]{0:T(1024)S...) while((s32[]{:T(128)}, ...), condition=%wide.region_7.7_spmd, body=%wide.region_4.6_spmd.sunk | while | flops 734522368 | bytes 154048688 | solution.py:92
  243.4 72.7 %all-reduce.10.cloned.1.call-done = bf16[2048,640]{1,0:T(8,128)(2,1)} async-done(((bf16[2048,640]{1,0:T(8,128)(2,1)}), bf16[2048,640]{1,0:T(8,128)(2,1)}) %all-reduce.10.cloned.1.call-update) | async-done | bytes 2621456 | tf_op jit(solution)/shard_map/psum | solution.py:187
  320.4 46.1 %all-gather.7.cloned.1.call-done = bf16[2,640,1280]{2,1,0:T(8,128)(2,1)} async-done(((bf16[2,40,1280]{2,1,0:T(8,128)(2,1)}), bf16[2,640,1280]{2,1,0:T(8,128)(2,1)}) %all-gather.7.cloned.1.call-update) | async-done | bytes 3276816 | tf_op jit(solution)/shard_map/all_gather | solution.py:165
  366.5 31.2 %multiply_convert_fusion.1 = (bf16[2048,1280]{1,0:T(8,128)(2,1)}, f32[2048,1280]{1,0:T(8,128)}, f32[2048,1280]{1,0:T(8,128)}) fusion(f32[1280]{0:T(1024)S(1)} %copy-done.52, bf16[2,640,1280]{2,1,0:T(8,128)(2,1)} %all-gather.7.cloned.1.call-done, f32[640]{0:T(1024)S(1)} %copy-done.73, f32[640]{0:T(1024)S(1)} %copy-done.51, f32[2048]{0:T(1024)S(1)} %fusion.84, ...), kind=kOutput, calls=%fused_computation.69 | convolution fusion | flops 3540254720 | bytes 33124864 | tf_op jit(solution)/shard_map/dot_general | solution.py:197
  436.2 54.0 %all-reduce.12.cloned.1.call-done = bf16[2048,640]{1,0:T(8,128)(2,1)} async-done(((bf16[2048,640]{1,0:T(8,128)(2,1)}), bf16[2048,640]{1,0:T(8,128)(2,1)}) %all-reduce.12.cloned.1.call-update) | async-done | bytes 2621456 | tf_op jit(solution)/shard_map/psum | solution.py:219
  500.1 60.7 %all-gather.9.cloned.1.call-done = bf16[4096,640]{1,0:T(8,128)(2,1)} async-done(((bf16[2048,640]{1,0:T(8,128)(2,1)}), bf16[4096,640]{1,0:T(8,128)(2,1)}) %all-gather.9.cloned.1.call-update) | async-done | bytes 5242896 | tf_op jit(solution)/shard_map/all_gather | solution.py:202
  580.6 277.4 %while.56 = (s32[]{:T(128)}, f32[2,1024,10,32]{1,3,2,0:T(8,128)}, f32[2,1024,10,32]{1,3,2,0:T(8,128)}, bf16[2,1024,10,32]{1,3,2,0:T(8,128)(2,1)}, bf16[2,1024,10...) while((s32[]{:T(128)}, f32[2,1024,10,32]{1,3,2,0:T(8,128)}, ...), condition=%wide.region_20.21_spmd, body=%wide.region_16.20_spmd.sunk | while | flops 1758686208 | bytes 284158464 | solution.py:235
  592.6 111.3 %while.58 = (s32[]{:T(128)}, f32[1024,10,32]{0,2,1:T(8,128)S(1)}, f32[1024,10,32]{0,2,1:T(8,128)}, f32[2,512,10,32]{1,3,2,0:T(8,128)}, bf16[2,512,10,32]{1,3,2,0...) while((s32[]{:T(128)}, f32[1024,10,32]{0,2,1:T(8,128)S(1)}, ...), condition=%wide.region_19.19_spmd.clone, body=%wide.region_17.18_spmd.clone.sunk | while | flops 1758686208 | bytes 255219920 | solution.py:110
  612.3 15.2 %multiply_reduce_fusion.13 = (f32[10,512]{1,0:T(8,128)S(1)}, f32[10,512,1024]{2,1,0:T(8,128)}) fusion(f32[10,512,1024]{2,1,0:T(8,128)} %copy-done, f32[10,512]{1,0:T(8,128)S(1)} %dynamic-slice_bitcast_fusion.15, pred[512,1024]{1,0:T(8,128)(4,1)S(1)} %broadcast_compare_fusion.4, bf16[1024,10,32]{0,2,1:T(8,128)(2,1)} %get-tuple-element.1032, ...), kind=kOutput, calls=%fused_computation.18.clone.1 | convolution fusion | flops 361753600 | bytes 43491332 | tf_op jit(solution)/shard_map/while/body/eval_jaxpr/while/body/eval_jaxpr/qhd,khd->hqk/dot_general | solution.py:69
  627.5 14.6 %multiply_convert_fusion.3 = bf16[10,512,1024]{2,1,0:T(8,128)(2,1)S(1)} fusion(f32[10,512,1024]{2,1,0:T(8,128)} %get-tuple-element.984, f32[10,512,1024]{2,1,0:T(8,128)} %copy-done, f32[10,512]{1,0:T(8,128)S(1)} %get-tuple-element.985, f32[10,512]{1,0:T(8,128)S(1)} %dynamic-slice_bitcast_fusion.15, pred[512,1024]{1,0:T(8,128)(4,1)S(1)} %broadcast_compare_fusion.4), kind=kLoop, calls=%fused_computation.17.clone.1 | loop fusion | flops 31457280 | bytes 52994048 | tf_op jit(solution)/shard_map/while/body/eval_jaxpr/while/body/eval_jaxpr/convert_element_type | solution.py:73
  668.1 15.2 %multiply_reduce_fusion.13 = (f32[10,512]{1,0:T(8,128)S(1)}, f32[10,512,1024]{2,1,0:T(8,128)}) fusion(f32[10,512,1024]{2,1,0:T(8,128)} %copy-done, f32[10,512]{1,0:T(8,128)S(1)} %dynamic-slice_bitcast_fusion.15, pred[512,1024]{1,0:T(8,128)(4,1)S(1)} %broadcast_compare_fusion.4, bf16[1024,10,32]{0,2,1:T(8,128)(2,1)} %get-tuple-element.1032, ...), kind=kOutput, calls=%fused_computation.18.clone.1 | convolution fusion | flops 361753600 | bytes 43491332 | tf_op jit(solution)/shard_map/while/body/eval_jaxpr/while/body/eval_jaxpr/qhd,khd->hqk/dot_general | solution.py:69
  683.3 14.6 %multiply_convert_fusion.3 = bf16[10,512,1024]{2,1,0:T(8,128)(2,1)S(1)} fusion(f32[10,512,1024]{2,1,0:T(8,128)} %get-tuple-element.984, f32[10,512,1024]{2,1,0:T(8,128)} %copy-done, f32[10,512]{1,0:T(8,128)S(1)} %get-tuple-element.985, f32[10,512]{1,0:T(8,128)S(1)} %dynamic-slice_bitcast_fusion.15, pred[512,1024]{1,0:T(8,128)(4,1)S(1)} %broadcast_compare_fusion.4), kind=kLoop, calls=%fused_computation.17.clone.1 | loop fusion | flops 31457280 | bytes 52994048 | tf_op jit(solution)/shard_map/while/body/eval_jaxpr/while/body/eval_jaxpr/convert_element_type | solution.py:73
  731.0 111.3 %while.58 = (s32[]{:T(128)}, f32[1024,10,32]{0,2,1:T(8,128)S(1)}, f32[1024,10,32]{0,2,1:T(8,128)}, f32[2,512,10,32]{1,3,2,0:T(8,128)}, bf16[2,512,10,32]{1,3,2,0...) while((s32[]{:T(128)}, f32[1024,10,32]{0,2,1:T(8,128)S(1)}, ...), condition=%wide.region_19.19_spmd.clone, body=%wide.region_17.18_spmd.clone.sunk | while | flops 1758686208 | bytes 255219920 | solution.py:110
  750.7 15.2 %multiply_reduce_fusion.13 = (f32[10,512]{1,0:T(8,128)S(1)}, f32[10,512,1024]{2,1,0:T(8,128)}) fusion(f32[10,512,1024]{2,1,0:T(8,128)} %copy-done, f32[10,512]{1,0:T(8,128)S(1)} %dynamic-slice_bitcast_fusion.15, pred[512,1024]{1,0:T(8,128)(4,1)S(1)} %broadcast_compare_fusion.4, bf16[1024,10,32]{0,2,1:T(8,128)(2,1)} %get-tuple-element.1032, ...), kind=kOutput, calls=%fused_computation.18.clone.1 | convolution fusion | flops 361753600 | bytes 43491332 | tf_op jit(solution)/shard_map/while/body/eval_jaxpr/while/body/eval_jaxpr/qhd,khd->hqk/dot_general | solution.py:69
  765.9 14.6 %multiply_convert_fusion.3 = bf16[10,512,1024]{2,1,0:T(8,128)(2,1)S(1)} fusion(f32[10,512,1024]{2,1,0:T(8,128)} %get-tuple-element.984, f32[10,512,1024]{2,1,0:T(8,128)} %copy-done, f32[10,512]{1,0:T(8,128)S(1)} %get-tuple-element.985, f32[10,512]{1,0:T(8,128)S(1)} %dynamic-slice_bitcast_fusion.15, pred[512,1024]{1,0:T(8,128)(4,1)S(1)} %broadcast_compare_fusion.4), kind=kLoop, calls=%fused_computation.17.clone.1 | loop fusion | flops 31457280 | bytes 52994048 | tf_op jit(solution)/shard_map/while/body/eval_jaxpr/while/body/eval_jaxpr/convert_element_type | solution.py:73
  806.5 15.2 %multiply_reduce_fusion.13 = (f32[10,512]{1,0:T(8,128)S(1)}, f32[10,512,1024]{2,1,0:T(8,128)}) fusion(f32[10,512,1024]{2,1,0:T(8,128)} %copy-done, f32[10,512]{1,0:T(8,128)S(1)} %dynamic-slice_bitcast_fusion.15, pred[512,1024]{1,0:T(8,128)(4,1)S(1)} %broadcast_compare_fusion.4, bf16[1024,10,32]{0,2,1:T(8,128)(2,1)} %get-tuple-element.1032, ...), kind=kOutput, calls=%fused_computation.18.clone.1 | convolution fusion | flops 361753600 | bytes 43491332 | tf_op jit(solution)/shard_map/while/body/eval_jaxpr/while/body/eval_jaxpr/qhd,khd->hqk/dot_general | solution.py:69
  821.6 14.6 %multiply_convert_fusion.3 = bf16[10,512,1024]{2,1,0:T(8,128)(2,1)S(1)} fusion(f32[10,512,1024]{2,1,0:T(8,128)} %get-tuple-element.984, f32[10,512,1024]{2,1,0:T(8,128)} %copy-done, f32[10,512]{1,0:T(8,128)S(1)} %get-tuple-element.985, f32[10,512]{1,0:T(8,128)S(1)} %dynamic-slice_bitcast_fusion.15, pred[512,1024]{1,0:T(8,128)(4,1)S(1)} %broadcast_compare_fusion.4), kind=kLoop, calls=%fused_computation.17.clone.1 | loop fusion | flops 31457280 | bytes 52994048 | tf_op jit(solution)/shard_map/while/body/eval_jaxpr/while/body/eval_jaxpr/convert_element_type | solution.py:73
  912.9 48.7 %all-reduce.14.cloned.1.call-done = bf16[2048,640]{1,0:T(8,128)(2,1)} async-done(((bf16[2048,640]{1,0:T(8,128)(2,1)}), bf16[2048,640]{1,0:T(8,128)(2,1)}) %all-reduce.14.cloned.1.call-update) | async-done | bytes 2621456 | tf_op jit(solution)/shard_map/psum | solution.py:248
  968.4 56.1 %all-reduce.3 = (f32[3,320]{1,0:T(4,128)S(1)}, f32[1280]{0:T(1024)S(1)}, f32[6,640]{1,0:T(8,128)S(1)}) all-reduce(f32[3,320]{1,0:T(4,128)S(1)} %convert_reduce_fusion.2, f32[1280]{0:T(1024)S(1)} %copy-done.68, f32[6,640]{1,0:T(8,128)S(1)} %stack.48), channel_id=1, replica_groups=mesh['dp'=16,'tp'=2] {'dp'}, use_global_device_ids=true, to_apply=%region_35.36 | all-reduce | flops 6080 | bytes 48640 | tf_op jit(solution)/shard_map/psum | solution.py:268
  1035.9 133.0 %all-reduce.16.cloned.1.call-done = (f32[4,640,320]{2,1,0:T(8,128)}, f32[2,640,1280]{2,1,0:T(8,128)}) async-done(((f32[4,640,320]{2,1,0:T(8,128)}, f32[2,640,1280]{2,1,0:T(8,128)}), (f32[4,640,320]{2,1,0:T(8,128)}, f32[2,640,1280]{2,1,0:T(8,128)})) %all-reduce.16.cloned.1.call-update) | async-done | bytes 9830416 | tf_op jit(solution)/shard_map/psum | solution.py:268
  1174.3 40.2 %all-reduce.2 = (f32[16]{0:T(128)S(1)}, f32[16]{0:T(128)S(1)}) all-reduce(f32[16]{0:T(128)S(1)} %concatenate.39, f32[16]{0:T(128)S(1)} %concatenate.37), channel_id=1, replica_groups=mesh['dp'=16,'tp'=2] {'dp','tp'}, use_global_device_ids=true, to_apply=%region_48.49 | all-reduce | flops 32 | bytes 256 | tf_op jit(solution)/shard_map/psum | solution.py:284
  (421 shorter events, 515.8 us)
Async XLA Ops:
  7.2 44.7 %all-gather.5.cloned.1.call-start = ((), (), s32[]{:S(2)}) async-start(), calls=%async_computation | async-start | bytes 2088960 | tf_op jit(solution)/shard_map/all_gather | solution.py:164
  9.1 307.0 %all-reduce.10.cloned.1.call-start = ((), (), s32[]{:S(2)}) async-start(), calls=%async_computation.1 | async-start | bytes 5242880 | tf_op jit(solution)/shard_map/psum | solution.py:187
  237.8 78.3 %copy-start.4 = (bf16[2048,640]{1,0:T(8,128)(2,1)S(1)}, bf16[2048,640]{1,0:T(8,128)(2,1)}, u32[]{:S(2)}) copy-start(bf16[2048,640]{1,0:T(8,128)(2,1)} %param.26) | copy-start | bytes 7864324
  237.8 78.3 %copy-start.43 = (f32[640]{0:T(1024)S(1)}, f32[640]{0:T(1024)}, u32[]{:S(2)}) copy-start(f32[640]{0:T(1024)} %get-tuple-element.569) | copy-start | bytes 7684
  242.6 123.9 %all-gather.7.cloned.1.call-start = ((), (), s32[]{:S(2)}) async-start(), calls=%async_computation.2 | async-start | bytes 3481600 | tf_op jit(solution)/shard_map/all_gather | solution.py:165
  243.4 246.9 %all-reduce.12.cloned.1.call-start = ((), (), s32[]{:S(2)}) async-start(), calls=%async_computation.3 | async-start | bytes 5242880 | tf_op jit(solution)/shard_map/psum | solution.py:219
  418.2 142.6 %all-gather.9.cloned.1.call-start = ((), (), s32[]{:S(2)}) async-start(), calls=%async_computation.5 | async-start | bytes 7864320 | tf_op jit(solution)/shard_map/all_gather | solution.py:202
  427.1 534.5 %all-reduce.14.cloned.1.call-start = ((), (), s32[]{:S(2)}) async-start(), calls=%async_computation.4 | async-start | bytes 5242880 | tf_op jit(solution)/shard_map/psum | solution.py:248
  887.1 281.8 %all-reduce.16.cloned.1.call-start = ((), (), s32[]{:S(2)}) async-start(), calls=%async_computation.6 | async-start | bytes 20971520 | tf_op jit(solution)/shard_map/psum | solution.py:268
  912.8 111.8 %copy-start.53 = (f32[1280]{0:T(1024)S(1)}, f32[1280]{0:T(1024)}, u32[]{:S(2)}) copy-start(f32[1280]{0:T(1024)} %param.32) | copy-start | bytes 15364
  912.8 111.8 %copy-start.66 = (f32[1280]{0:T(1024)S(1)}, f32[1280]{0:T(1024)}, u32[]{:S(2)}) copy-start(f32[1280]{0:T(1024)} %param.37) | copy-start | bytes 15364
  912.8 111.8 %copy-start.67 = (f32[1280]{0:T(1024)S(1)}, f32[1280]{0:T(1024)}, u32[]{:S(2)}) copy-start(f32[1280]{0:T(1024)} %param.42) | copy-start | bytes 15364
  912.8 114.3 %copy-start.42 = (f32[6,640]{1,0:T(8,128)S(1)}, f32[6,640]{1,0:T(8,128)}, u32[]{:S(2)}) copy-start(f32[6,640]{1,0:T(8,128)} %param.33) | copy-start | bytes 46084
  912.8 114.3 %copy-start.59 = (f32[6,640]{1,0:T(8,128)S(1)}, f32[6,640]{1,0:T(8,128)}, u32[]{:S(2)}) copy-start(f32[6,640]{1,0:T(8,128)} %param.38) | copy-start | bytes 46084
  912.8 114.2 %copy-start.60 = (f32[6,640]{1,0:T(8,128)S(1)}, f32[6,640]{1,0:T(8,128)}, u32[]{:S(2)}) copy-start(f32[6,640]{1,0:T(8,128)} %param.43) | copy-start | bytes 46084
  912.8 115.6 %copy-start.58 = (f32[3,320]{1,0:T(4,128)S(1)}, f32[3,320]{1,0:T(4,128)}, u32[]{:S(2)}) copy-start(f32[3,320]{1,0:T(4,128)} %param.31) | copy-start | bytes 11524
  912.9 115.6 %copy-start.69 = (f32[3,320]{1,0:T(4,128)S(1)}, f32[3,320]{1,0:T(4,128)}, u32[]{:S(2)}) copy-start(f32[3,320]{1,0:T(4,128)} %param.36) | copy-start | bytes 11524
  912.9 115.6 %copy-start.70 = (f32[3,320]{1,0:T(4,128)S(1)}, f32[3,320]{1,0:T(4,128)}, u32[]{:S(2)}) copy-start(f32[3,320]{1,0:T(4,128)} %param.41) | copy-start | bytes 11524
  1030.3 138.7 %copy-start.31 = (f32[4,40,320]{2,1,0:T(8,128)S(1)}, f32[4,40,320]{2,1,0:T(8,128)}, u32[]{:S(2)}) copy-start(f32[4,40,320]{2,1,0:T(8,128)} %param.29) | copy-start | bytes 614404
  1030.3 138.7 %copy-start.39 = (f32[4,40,320]{2,1,0:T(8,128)S(1)}, f32[4,40,320]{2,1,0:T(8,128)}, u32[]{:S(2)}) copy-start(f32[4,40,320]{2,1,0:T(8,128)} %param.34) | copy-start | bytes 614404
  1030.3 140.0 %copy-start.24 = (f32[2,40,1280]{2,1,0:T(8,128)S(1)}, f32[2,40,1280]{2,1,0:T(8,128)}, u32[]{:S(2)}) copy-start(f32[2,40,1280]{2,1,0:T(8,128)} %param.30) | copy-start | bytes 1228804
  1035.9 185.5 %copy-start.54 = (f32[1280]{0:T(1024)S(1)}, f32[1280]{0:T(1024)}, u32[]{:S(2)}) copy-start(f32[1280]{0:T(1024)} %param.32) | copy-start | bytes 15364
  1035.9 185.5 %copy-start.55 = (f32[1280]{0:T(1024)S(1)}, f32[1280]{0:T(1024)}, u32[]{:S(2)}) copy-start(f32[1280]{0:T(1024)} %get-tuple-element.659) | copy-start | bytes 15364
  1035.9 185.5 %copy-start.56 = (f32[1280]{0:T(1024)S(1)}, f32[1280]{0:T(1024)}, u32[]{:S(2)}) copy-start(f32[1280]{0:T(1024)} %get-tuple-element.660) | copy-start | bytes 15364
  (78 other events, 1347.1 us)
Sparse Core Ops, SparseCore 0:
  10.9 40.9 all-gather.4
  242.7 73.3 all-reduce.9
  319.1 47.3 all-gather.6
  418.4 71.8 all-reduce.11
  492.2 68.5 all-gather.8
  887.2 74.3 all-reduce.13
  965.9 202.9 all-reduce.15
